TPU v7x, 256 devices: a whole 4x4x8 slice. The times are simulated.
256 devices in a mesh: shard: 32 (over z, x), tensor: 4 (over y), section: 2 (over core).
Axes of the slice: x: 4, y: 4, z: 8, core: 2. Of those that a mesh axis runs over, the one named last changes fastest.
Arguments:
- grad_parts: bfloat16 [8, 32, 1024, 1024], P(('tensor', 'section'), None, 'shard')
- weights: bfloat16 [32, 1024, 1024], P(None, 'shard', ('tensor', 'section')), may hold values from -6 to 6
- adam_m: float32 [32, 1024, 1024], P(None, 'shard', ('tensor', 'section'))
- adam_v: float32 [32, 1024, 1024], P(None, 'shard', ('tensor', 'section')), may hold values from 0.01 to 1
- left_stat: float32 [96, 1024, 1024], P('shard', None, ('tensor', 'section')), may hold values from -18 to 18
- right_stat: float32 [96, 1024, 1024], P('shard', None, ('tensor', 'section')), may hold values from -18 to 18
- left_root: bfloat16 [32, 1024, 1024], P(None, 'shard', ('tensor', 'section')), as said below
- right_root: bfloat16 [32, 1024, 1024], P(None, 'shard', ('tensor', 'section')), as said below
- block_owner: int32 [32], replicated, may hold values from 0 to 31, as said below
- block_matrix: int32 [32], replicated, may hold values from 0 to 4, as said below
- factors: float32 [832, 2048], P('shard', ('tensor', 'section')), may hold values from -6 to 6
- factor_grad: bfloat16 [832, 2048], P('shard', ('tensor', 'section')), may hold values from -6 to 6
- factor_m: float32 [832, 2048], P('shard', ('tensor', 'section')), may hold values from -3 to 3
- factor_v: float32 [832, 2048], P('shard', ('tensor', 'section')), may hold values from 0.2 to 2
Outputs:
- new_weights: bfloat16 [32, 1024, 1024], P(None, 'shard')
- adam_m_new: float32 [32, 1024, 1024], P(None, 'shard', ('tensor', 'section'))
- adam_v_new: float32 [32, 1024, 1024], P(None, 'shard', ('tensor', 'section'))
- left_new: float32 [96, 1024, 1024], P('shard', None, ('tensor', 'section'))
- right_new: float32 [96, 1024, 1024], P('shard', None, ('tensor', 'section'))
- factors_new: float32 [832, 2048], P('shard', ('tensor', 'section'))
- factor_m_new: float32 [832, 2048], P('shard', ('tensor', 'section'))
- factor_v_new: float32 [832, 2048], P('shard', ('tensor', 'section'))
Inputs may be any that keep to these rules, and one draw needn't show every extreme that they name: `block_owner`: no owner holds more than 3 blocks, and some owner holds exactly 3. `block_matrix`: matrices 0 to 3 hold 4 blocks each, all other blocks belong to matrix 4. `left_root`: every block is symmetric. `right_root`: every block is symmetric.
All inputs are finite; a program needn't handle non-finite values.
Results may differ from a plain program's by a relative error of at most 0.014.
Values may be sent and summed in bfloat16 or wider, within the bound.
A program may use at most 128 MiB of HBM per device.

v0:
```python
import jax
import jax.numpy as jnp
from jax import lax
from jax.sharding import PartitionSpec as P

B = 1024
MATS = 5
BETA_ONE = 0.9
BETA_TWO = 0.95
BETA_STAT = 0.95
LEARNING = 0.1
DECAY_RATE = 0.1
EPSILON = 1e-08
FLOOR_RATE = 1e-06
CORRECT_ONE = 1.0 - 0.9**10
CORRECT_TWO = 1.0 - 0.95**10


def adam_direction(grad_float, moment, second):
    moment_new = BETA_ONE * moment + (1.0 - BETA_ONE) * grad_float
    second_new = BETA_TWO * second + (1.0 - BETA_TWO) * grad_float * grad_float
    direction = moment_new / CORRECT_ONE / (jnp.sqrt(second_new / CORRECT_TWO) + EPSILON)
    return (moment_new, second_new, direction)


def slot_numbers(block_owner, capacity):
    positions = jnp.arange(block_owner.shape[0], dtype=jnp.int32)
    earlier = (block_owner[:, None] == block_owner[None, :]) & (
        positions[None, :] < positions[:, None]
    )
    return block_owner * capacity + jnp.sum(earlier.astype(jnp.int32), axis=1)


def slot_contents(slot, slot_total):
    positions = jnp.arange(slot.shape[0], dtype=jnp.int32)
    matches = jnp.arange(slot_total, dtype=jnp.int32)[:, None] == slot[None, :]
    occupied = jnp.any(matches, axis=1)
    block_ids = jnp.sum(jnp.where(matches, positions[None, :], 0), axis=1)
    return (block_ids, occupied)


def fill_slots(tiles, block_ids, occupied):
    picked = jnp.take(tiles, block_ids, axis=0)
    return jnp.where(occupied[:, None, None], picked, jnp.zeros_like(picked))


def shards(
    grad_parts,
    weights,
    adam_m,
    adam_v,
    left_stat,
    right_stat,
    left_root,
    right_root,
    block_owner,
    block_matrix,
    factors,
    factor_grad,
    factor_m,
    factor_v,
):
    capacity = left_stat.shape[0]
    owners = lax.axis_size("shard")
    owner_index = lax.axis_index("shard")
    group_index = lax.axis_index(("tensor", "section"))
    partials = grad_parts[0].astype(jnp.float32)
    gradient = lax.psum_scatter(
        partials.astype(jnp.bfloat16), ("tensor", "section"), scatter_dimension=2, tiled=True
    )
    gradient = lax.optimization_barrier(gradient)
    grad_float = gradient.astype(jnp.float32)
    adam_m_new, adam_v_new, direction = adam_direction(grad_float, adam_m, adam_v)
    matrix_range = jnp.arange(MATS, dtype=jnp.int32)
    onehot = (block_matrix[:, None] == matrix_range[None, :]).astype(jnp.float32)
    adam_part = jnp.sum(jnp.sum(direction * direction, axis=(1, 2))[:, None] * onehot, axis=0)
    slot = slot_numbers(block_owner, capacity)
    block_ids, occupied = slot_contents(slot, owners * capacity)
    slab_width = gradient.shape[2]

    def to_block(x):
        return lax.all_to_all(x, "shard", split_axis=0, concat_axis=1, tiled=True)

    left_cols = to_block(left_root)
    right_cols = to_block(right_root)
    left_full = lax.all_gather(left_cols, ("tensor", "section"), axis=2, tiled=True)
    grad_cols = to_block(gradient)
    mixed = jnp.einsum(
        "sij,sjc->sic", left_full, grad_cols, preferred_element_type=jnp.float32
    ).astype(jnp.bfloat16)
    mixed_full = lax.all_gather(mixed, ("tensor", "section"), axis=2, tiled=True)
    precond = jnp.einsum("sik,skc->sic", mixed_full, right_cols, preferred_element_type=jnp.float32)
    own_matrix = lax.dynamic_slice_in_dim(block_matrix, owner_index, 1)
    own_onehot = (own_matrix == matrix_range).astype(jnp.float32)
    shampoo_part = jnp.sum(precond * precond) * own_onehot
    precond_tile = lax.all_to_all(
        precond.astype(jnp.bfloat16), "shard", split_axis=1, concat_axis=0, tiled=True
    ).astype(jnp.float32)
    slot_cols = to_block(fill_slots(gradient, block_ids, occupied))
    grad_full = lax.all_gather(slot_cols, ("tensor", "section"), axis=2, tiled=True)
    first_row = group_index * slab_width
    grad_rows_own = lax.dynamic_slice_in_dim(grad_full, first_row, slab_width, 1)
    gram_left = jnp.einsum(
        "sik,sjk->sij", grad_full, grad_rows_own, preferred_element_type=jnp.float32
    )
    gram_right = jnp.einsum(
        "ski,skj->sij", grad_full, slot_cols, preferred_element_type=jnp.float32
    )
    left_new = BETA_STAT * left_stat + (1.0 - BETA_STAT) * gram_left
    right_new = BETA_STAT * right_stat + (1.0 - BETA_STAT) * gram_right
    adam_norm, shampoo_norm = lax.psum((adam_part, shampoo_part), ("shard", "tensor", "section"))
    counts = jnp.sum(onehot, axis=0) * float(B * B)
    graft_scale = jnp.sqrt(adam_norm / (shampoo_norm + FLOOR_RATE * counts))
    block_scale = jnp.sum(onehot * graft_scale[None, :], axis=1)
    weights_float = weights.astype(jnp.float32)
    updated = (
        weights_float
        - LEARNING * (block_scale[:, None, None] * precond_tile + DECAY_RATE * weights_float)
    ).astype(jnp.bfloat16)
    factor_m_new, factor_v_new, factor_step = adam_direction(
        factor_grad.astype(jnp.float32), factor_m, factor_v
    )
    factors_new = factors - LEARNING * (factor_step + DECAY_RATE * factors)
    new_weights = lax.all_gather(updated, ("tensor", "section"), axis=2, tiled=True)
    return (
        new_weights,
        adam_m_new,
        adam_v_new,
        left_new,
        right_new,
        factors_new,
        factor_m_new,
        factor_v_new,
    )


def solution(mesh):
    in_specs = (
        P(("tensor", "section"), None, "shard", None),
        P(None, "shard", ("tensor", "section")),
        P(None, "shard", ("tensor", "section")),
        P(None, "shard", ("tensor", "section")),
        P("shard", None, ("tensor", "section")),
        P("shard", None, ("tensor", "section")),
        P(None, "shard", ("tensor", "section")),
        P(None, "shard", ("tensor", "section")),
        P(),
        P(),
        P("shard", ("tensor", "section")),
        P("shard", ("tensor", "section")),
        P("shard", ("tensor", "section")),
        P("shard", ("tensor", "section")),
    )
    out_specs = (
        P(None, "shard", None),
        P(None, "shard", ("tensor", "section")),
        P(None, "shard", ("tensor", "section")),
        P("shard", None, ("tensor", "section")),
        P("shard", None, ("tensor", "section")),
        P("shard", ("tensor", "section")),
        P("shard", ("tensor", "section")),
        P("shard", ("tensor", "section")),
    )
    return jax.shard_map(shards, mesh=mesh, in_specs=in_specs, out_specs=out_specs, check_vma=False)
```

profile of v0, /device:TPU:1, one launch (start us, length us, event | category | flops | bytes accessed | tf_op | source)
XLA Modules:
  0.0 326.8 jit_solution(6027712454618299210)
XLA Ops:
  7.2 0.0 reduce-scatter.4.cloned.1.call-start
  7.2 12.5 %copy.31 = bf16[32,32,1024]{1,0,2:T(8,128)(2,1)} copy(bf16[32,32,1024]{2,1,0:T(8,128)(2,1)} %bitcast.39) | data formatting | bytes 4194304
  19.7 12.4 %reshape.91 = bf16[1024,1024]{1,0:T(8,128)(2,1)} reshape(bf16[1024,32,32]{2,1,0:T(8,128)(2,1)} %bitcast.34) | data formatting | bytes 4194304
  32.1 0.0 reduce-scatter.4.cloned.1.call-update
  32.1 0.0 all-gather.6.cloned.1.call-start
  32.2 0.9 copy-done.5
  33.1 23.1 %all_to_all.57 = bf16[32,32,128]{2,1,0:T(8,128)(2,1)} all-to-all(bf16[32,32,128]{2,1,0:T(8,128)(2,1)S(1)} %copy-done.5), channel_id=1, replica_groups=mesh['shard'=32,'tensor'=4,'section'=2] {'shard'}, dimensions={0} | all-to-all | bytes 524288 | tf_op jit(solution)/shard_map/all_to_all | solution.py:82
  56.1 0.0 all-gather.6.cloned.1.call-update
  56.1 14.5 %reduce-scatter.4.cloned.1.call-done = bf16[128,1024]{1,0:T(8,128)(2,1)} async-done(((bf16[1024,1024]{1,0:T(8,128)(2,1)}), bf16[128,1024]{1,0:T(8,128)(2,1)}) %reduce-scatter.4.cloned.1.call-update) | async-done | bytes 262160
  70.6 1.8 reshape.92
  72.5 1.8 copy.32
  74.2 9.1 %all-to-all-start.1 = ((bf16[32,32,128]{2,1,0:T(8,128)(2,1)}), bf16[32,32,128]{2,1,0:T(8,128)(2,1)S(1)}, u32[]{:S(2)}, u32[]{:S(2)}) async-start(bf16[32,32,128]{2,1,0:T(8,128)(2,1)} %copy.32), calls=%async_computation.1 | async-start | bytes 524288 | tf_op jit(solution)/shard_map/all_to_all | solution.py:82
  83.3 0.0 all-gather.12.cloned.1.call-start
  83.4 19.8 %all-gather.6.cloned.1.call-done = bf16[1,1024,1024]{2,1,0:T(8,128)(2,1)} async-done(((bf16[1,1024,128]{2,1,0:T(8,128)(2,1)}), bf16[1,1024,1024]{2,1,0:T(8,128)(2,1)}) %all-gather.6.cloned.1.call-update) | async-done | bytes 2097168 | tf_op jit(solution)/shard_map/all_gather | solution.py:86
  103.2 3.0 fusion.2
  106.2 0.0 all-gather.12.cloned.1.call-update
  106.2 9.5 %all-to-all-start.2 = ((bf16[32,32,128]{2,1,0:T(8,128)(2,1)}), bf16[32,32,128]{2,1,0:T(8,128)(2,1)S(1)}, u32[]{:S(2)}, u32[]{:S(2)}) async-start(bf16[32,32,128]{2,1,0:T(8,128)(2,1)} %param.21), calls=%async_computation.2 | async-start | bytes 524288 | tf_op jit(solution)/shard_map/all_to_all | solution.py:82
  115.8 0.6 dynamic_slice.6
  116.4 2.3 multiply_reduce_fusion.1
  118.7 8.8 %all-to-all-done.2 = bf16[32,32,128]{2,1,0:T(8,128)(2,1)S(1)} async-done(((bf16[32,32,128]{2,1,0:T(8,128)(2,1)}), bf16[32,32,128]{2,1,0:T(8,128)(2,1)S(1)}, u32[]{:S(2)}, u32[]{:S(2)}) %all-to-all-start.2) | async-done | bytes 262176 | tf_op jit(solution)/shard_map/all_to_all | solution.py:82
  127.4 9.2 %all-gather.12.cloned.1.call-done = bf16[1024,1024]{1,0:T(8,128)(2,1)} async-done(((bf16[1024,128]{1,0:T(8,128)(2,1)}), bf16[1024,1024]{1,0:T(8,128)(2,1)}) %all-gather.12.cloned.1.call-update) | async-done | bytes 2097168 | tf_op jit(solution)/shard_map/all_gather | solution.py:91
  136.6 2.9 multiply_reduce_fusion
  139.5 0.4 copy.34
  140.0 0.5 broadcast.81
  140.5 2.2 reduce.2
  142.7 0.8 reshape.93
  143.5 9.5 %all-to-all-start.3 = ((bf16[32,2,2048]{2,1,0:T(2,128)(2,1)}), bf16[32,2,2048]{2,1,0:T(2,128)(2,1)S(1)}, u32[]{:S(2)}, u32[]{:S(2)}) async-start(bf16[32,2,2048]{2,1,0:T(2,128)(2,1)} %reshape.93), calls=%async_computation.3 | async-start | bytes 524288 | tf_op jit(solution)/shard_map/all_to_all | solution.py:96
  153.0 0.0 all-gather.8.cloned.1.call-start
  153.1 0.1 convert_reduce_fusion.1
  153.2 1.3 compare_select_fusion.2
  154.5 76.9 %all-reduce = (f32[5]{0:T(128)S(1)}, f32[5]{0:T(128)S(1)}) all-reduce(f32[5]{0:T(128)S(1)} %get-tuple-element.9, f32[5]{0:T(128)S(1)} %compare_select_fusion.2), channel_id=1, replica_groups=mesh['shard'=32,'tensor'=4,'section'=2] {'shard','tensor','section'}, use_global_device_ids=true, to_apply=%region_3.0 | all-reduce | flops 10 | bytes 80 | tf_op jit(solution)/shard_map/psum | solution.py:111
  231.4 0.1 select_reduce_fusion.1
  231.5 0.3 reshape.94
  231.8 0.5 bitcast_convert_fusion
  232.4 0.9 fusion.8
  233.3 0.0 all-gather.10.cloned.1.call-start
  233.3 0.2 convert_reduce_fusion
  233.5 0.1 select_reduce_fusion
  233.6 0.1 fusion.13
  233.7 1.7 gather_fusion
  235.4 0.3 select_select_fusion
  235.7 27.4 %all_to_all.58 = bf16[96,32,128]{2,1,0:T(8,128)(2,1)S(1)} all-to-all(bf16[96,32,128]{2,1,0:T(8,128)(2,1)S(1)} %select_select_fusion), channel_id=1, replica_groups=mesh['shard'=32,'tensor'=4,'section'=2] {'shard'}, dimensions={0} | all-to-all | bytes 1572864 | tf_op jit(solution)/shard_map/all_to_all | solution.py:82
  263.1 1.0 copy.28
  264.1 0.7 multiply_subtract_fusion
  264.8 44.7 %all-gather.10.cloned.1.call-done = bf16[3,1024,1024]{2,1,0:T(8,128)(2,1)} async-done(((bf16[3,1024,128]{2,1,0:T(8,128)(2,1)}), bf16[3,1024,1024]{2,1,0:T(8,128)(2,1)}) %all-gather.10.cloned.1.call-update) | async-done | bytes 6291472 | tf_op jit(solution)/shard_map/all_gather | solution.py:100
  309.5 6.5 %multiply_add_fusion = f32[3,1024,128]{2,1,0:T(8,128)} fusion(f32[3,1024,128]{2,1,0:T(8,128)S(1)} %copy-done.2, bf16[3,1024,1024]{2,1,0:T(8,128)(2,1)} %all-gather.10.cloned.1.call-done, bf16[3,1024,128]{2,1,0:T(8,128)(2,1)} %bitcast.36), kind=kOutput, calls=%fused_computation.3 | convolution fusion | flops 806486016 | bytes 10223616 | tf_op jit(solution)/shard_map/ski,skj->sij/dot_general | solution.py:106
  316.0 2.9 multiply_add_fusion.1
  319.0 1.3 copy.36
  (37 shorter events, 0.1 us)
Async XLA Ops:
  7.2 63.4 %reduce-scatter.4.cloned.1.call-start = ((), (), s32[]{:S(2)}) async-start(), calls=%async_computation.10 | async-start | bytes 2359296
  32.1 0.9 copy-start.5
  32.1 71.0 %all-gather.6.cloned.1.call-start = ((), (), s32[]{:S(2)}) async-start(), calls=%async_computation.6 | async-start | bytes 2359296 | tf_op jit(solution)/shard_map/all_gather | solution.py:86
  74.2 41.5 %copy-start.11 = (s32[32]{0:T(128)S(1)}, s32[32]{0:T(128)}, u32[]{:S(2)}) copy-start(s32[32]{0:T(128)} %param.23) | copy-start | bytes 388
  74.2 42.1 %copy-start.3 = (f32[32,32,128]{2,1,0:T(8,128)S(1)}, f32[32,32,128]{2,1,0:T(8,128)}, u32[]{:S(2)}) copy-start(f32[32,32,128]{2,1,0:T(8,128)} %param.16) | copy-start | bytes 1572868
  74.2 42.1 %copy-start.4 = (f32[32,32,128]{2,1,0:T(8,128)S(1)}, f32[32,32,128]{2,1,0:T(8,128)}, u32[]{:S(2)}) copy-start(f32[32,32,128]{2,1,0:T(8,128)} %param.17) | copy-start | bytes 1572868
  74.2 28.9 %all-to-all-start.1 = ((bf16[32,32,128]{2,1,0:T(8,128)(2,1)}), bf16[32,32,128]{2,1,0:T(8,128)(2,1)S(1)}, u32[]{:S(2)}, u32[]{:S(2)}) async-start(bf16[32,32,128]{2,1,0:T(8,128)(2,1)} %copy.32), calls=%async_computation.1 | async-start | bytes 524288 | tf_op jit(solution)/shard_map/all_to_all | solution.py:82
  83.3 53.3 %all-gather.12.cloned.1.call-start = ((), (), s32[]{:S(2)}) async-start(), calls=%async_computation.9 | async-start | bytes 2359296 | tf_op jit(solution)/shard_map/all_gather | solution.py:91
  106.2 21.2 %all-to-all-start.2 = ((bf16[32,32,128]{2,1,0:T(8,128)(2,1)}), bf16[32,32,128]{2,1,0:T(8,128)(2,1)S(1)}, u32[]{:S(2)}, u32[]{:S(2)}) async-start(bf16[32,32,128]{2,1,0:T(8,128)(2,1)} %param.21), calls=%async_computation.2 | async-start | bytes 524288 | tf_op jit(solution)/shard_map/all_to_all | solution.py:82
  139.5 92.8 %copy-start.6 = (bf16[32,32,128]{2,1,0:T(8,128)(2,1)S(1)}, bf16[32,32,128]{2,1,0:T(8,128)(2,1)}, u32[]{:S(2)}) copy-start(bf16[32,32,128]{2,1,0:T(8,128)(2,1)} %param.15) | copy-start | bytes 786436
  142.7 90.6 %copy-start.13 = (s32[32]{0:T(128)S(1)}, s32[32]{0:T(128)}, u32[]{:S(2)}) copy-start(s32[32]{0:T(128)} %param.22) | copy-start | bytes 388
  143.5 88.0 %all-to-all-start.3 = ((bf16[32,2,2048]{2,1,0:T(2,128)(2,1)}), bf16[32,2,2048]{2,1,0:T(2,128)(2,1)S(1)}, u32[]{:S(2)}, u32[]{:S(2)}) async-start(bf16[32,2,2048]{2,1,0:T(2,128)(2,1)} %reshape.93), calls=%async_computation.3 | async-start | bytes 524288 | tf_op jit(solution)/shard_map/all_to_all | solution.py:96
  153.0 111.8 %all-gather.8.cloned.1.call-start = ((), (), s32[]{:S(2)}) async-start(), calls=%async_computation.7 | async-start | bytes 2359296 | tf_op jit(solution)/shard_map/all_gather | solution.py:124
  233.3 76.2 %all-gather.10.cloned.1.call-start = ((), (), s32[]{:S(2)}) async-start(), calls=%async_computation.8 | async-start | bytes 7077888 | tf_op jit(solution)/shard_map/all_gather | solution.py:100
  235.7 28.4 %copy-start.7 = (f32[26,256]{1,0:T(8,128)S(1)}, f32[26,256]{1,0:T(8,128)}, u32[]{:S(2)}) copy-start(f32[26,256]{1,0:T(8,128)} %param.24) | copy-start | bytes 79876
  235.7 28.4 %copy-start.8 = (f32[26,256]{1,0:T(8,128)S(1)}, f32[26,256]{1,0:T(8,128)}, u32[]{:S(2)}) copy-start(f32[26,256]{1,0:T(8,128)} %param.26) | copy-start | bytes 79876
  235.7 28.4 %copy-start.9 = (f32[26,256]{1,0:T(8,128)S(1)}, f32[26,256]{1,0:T(8,128)}, u32[]{:S(2)}) copy-start(f32[26,256]{1,0:T(8,128)} %param.27) | copy-start | bytes 79876
  235.7 28.4 %copy-start.10 = (bf16[26,256]{1,0:T(8,128)(2,1)S(1)}, bf16[26,256]{1,0:T(8,128)(2,1)}, u32[]{:S(2)}) copy-start(bf16[26,256]{1,0:T(8,128)(2,1)} %param.25) | copy-start | bytes 39940
  235.7 73.7 %copy-start.2 = (f32[3,1024,128]{2,1,0:T(8,128)S(1)}, f32[3,1024,128]{2,1,0:T(8,128)}, u32[]{:S(2)}) copy-start(f32[3,1024,128]{2,1,0:T(8,128)} %param.19) | copy-start | bytes 4718596
  264.8 51.2 %copy-start.12 = (f32[3,1024,128]{2,1,0:T(8,128)S(1)}, f32[3,1024,128]{2,1,0:T(8,128)}, u32[]{:S(2)}) copy-start(f32[3,1024,128]{2,1,0:T(8,128)} %param.18) | copy-start | bytes 4718596
  309.5 6.5 %copy-start = (bf16[3,1024,1024]{2,1,0:T(8,128)(2,1)S(1)}, bf16[3,1024,1024]{2,1,0:T(8,128)(2,1)}, u32[]{:S(2)}) copy-start(bf16[3,1024,1024]{2,1,0:T(8,128)(2,1)} %all-gather.10.cloned.1.call-done) | copy-start | bytes 18874372
  316.0 3.0 copy-start.1
Sparse Core Ops, SparseCore 0:
  32.3 38.3 reduce-scatter.3
  72.4 30.6 all-gather.5
  106.3 30.2 all-gather.11
  233.4 25.8 all-gather.7
  264.2 45.2 all-gather.9
where the time goes:
time: 328 us; the launch traced here: 327 us
  blocking collectives  127 us (39%)
  waiting for transfers between devices  97 us (30%)
  local copies, waits for them, and re-layouts  35.9 us (11%)
  starting transfers between devices  28.4 us (9%)
  matrix products  15.4 us (5%)
  between operations  14 us (4%)
  other arithmetic  8.81 us (3%)
    psum x1, blocking collectives, shards(): lax.psum((adam_part, shampoo_part), ('shard', 'tensor', 'section'))  76.9 us
    all_to_all x2, blocking collectives, to_block(): return lax.all_to_all(x, 'shard', split_axis=0, concat_axis=1, tiled=True)  50.4 us
    all_gather x1, waiting for transfers between devices, shards(): lax.all_gather(slot_cols, ('tensor', 'section'), axis=2, tiled=True)  44.7 us
    unnamed x36, local copies, waits for them, and re-layouts  32.3 us
    all_gather x1, waiting for transfers between devices, shards(): lax.all_gather(left_cols, ('tensor', 'section'), axis=2, tiled=True)  19.8 us
    all_to_all x2, starting transfers between devices, to_block(): return lax.all_to_all(x, 'shard', split_axis=0, concat_axis=1, tiled=True)  18.6 us
    unnamed x6, waiting for transfers between devices  14.6 us
    all_to_all x1, starting transfers between devices, shards(): lax.all_to_all(precond.astype(jnp.bfloat16), 'shard', split_axis=1, conca...  9.54 us
  transfers between devices with their start and end apart: 8, of which 5 were waited for; matrix products, arithmetic and copies ran while one was open for 4% of the time, Pallas kernels for 0%

commit v1 on v0

--- a/solution.py
+++ b/solution.py
@@ -97,7 +97,15 @@
         precond.astype(jnp.bfloat16), "shard", split_axis=1, concat_axis=0, tiled=True
     ).astype(jnp.float32)
     slot_cols = to_block(fill_slots(gradient, block_ids, occupied))
-    grad_full = lax.all_gather(slot_cols, ("tensor", "section"), axis=2, tiled=True)
+    grad_full = jnp.concatenate(
+        lax.all_to_all(
+            jnp.stack([slot_cols] * lax.axis_size(("tensor", "section"))),
+            ("tensor", "section"),
+            0,
+            0,
+        ),
+        axis=2,
+    )
     first_row = group_index * slab_width
     grad_rows_own = lax.dynamic_slice_in_dim(grad_full, first_row, slab_width, 1)
     gram_left = jnp.einsum(

time: 328 us -> 355 us (1.082)
  blocking collectives: 127 us -> 155 us
  waiting for transfers between devices: 97 us -> 77.4 us
  starting transfers between devices: 28.4 us -> 38.2 us
  local copies, waits for them, and re-layouts: 35.9 us -> 44.7 us
    psum x1, blocking collectives: 76.9 us -> 131 us  [shards(): lax.psum((adam_part, shampoo_part), ('shard', 'tensor', 'section'))]
    all_gather x1 -> x0, waiting for transfers between devices: 44.7 us -> none  [shards(): lax.all_gather(slot_cols, ('tensor', 'section'), axis=2, tiled=True)]
    all_to_all x2 -> x1, blocking collectives: 50.4 us -> 23.1 us  [to_block(): return lax.all_to_all(x, 'shard', split_axis=0, concat_axis=1, tiled=True)]
    all_gather x1, waiting for transfers between devices: 0.01 us -> 10.6 us  [shards(): lax.all_gather(updated, ('tensor', 'section'), axis=2, tiled=True)]
    all_to_all x1, waiting for transfers between devices: 0.01 us -> 10.2 us  [shards(): lax.all_to_all(precond.astype(jnp.bfloat16), 'shard', split_axis=1, conca...]
    all_to_all x2 -> x3, waiting for transfers between devices: 8.75 us -> 17.6 us  [to_block(): return lax.all_to_all(x, 'shard', split_axis=0, concat_axis=1, tiled=True)]
    all_to_all x0 -> x1, starting transfers between devices: none -> 8.52 us  [shards(): lax.all_to_all(jnp.stack([slot_cols] * lax.axis_size(('tensor', 'section'...]
    all_gather x1, waiting for transfers between devices: 9.22 us -> 4.71 us  [shards(): lax.all_gather(mixed, ('tensor', 'section'), axis=2, tiled=True)]
  transfers between devices with their start and end apart: 8 -> 9, of which waited for: 5 -> 7; matrix products, arithmetic and copies ran while one was open for 4% -> 10% of each run, Pallas kernels for 0% -> 0%
where the time goes in v1:
time: 355 us; the launch traced here: 354 us
  blocking collectives  155 us (44%)
  waiting for transfers between devices  77.4 us (22%)
  local copies, waits for them, and re-layouts  44.7 us (13%)
  starting transfers between devices  38.2 us (11%)
  matrix products  15.1 us (4%)
  between operations  14 us (4%)
  other arithmetic  9.74 us (3%)
    psum x1, blocking collectives, shards(): lax.psum((adam_part, shampoo_part), ('shard', 'tensor', 'section'))  131 us
    unnamed x32, local copies, waits for them, and re-layouts  34.2 us
    all_to_all x3, starting transfers between devices, to_block(): return lax.all_to_all(x, 'shard', split_axis=0, concat_axis=1, tiled=True)  23.2 us
    all_to_all x1, blocking collectives, to_block(): return lax.all_to_all(x, 'shard', split_axis=0, concat_axis=1, tiled=True)  23.1 us
    all_gather x1, waiting for transfers between devices, shards(): lax.all_gather(left_cols, ('tensor', 'section'), axis=2, tiled=True)  19.8 us
    all_to_all x3, waiting for transfers between devices, to_block(): return lax.all_to_all(x, 'shard', split_axis=0, concat_axis=1, tiled=True)  17.6 us
    unnamed x5, waiting for transfers between devices  14.5 us
    all_gather x1, waiting for transfers between devices, shards(): lax.all_gather(updated, ('tensor', 'section'), axis=2, tiled=True)  10.6 us
  transfers between devices with their start and end apart: 9, of which 7 were waited for; matrix products, arithmetic and copies ran while one was open for 10% of the time, Pallas kernels for 0%

profile of v1, /device:TPU:1, one launch (start us, length us, event | category | flops | bytes accessed | tf_op | source)
XLA Modules:
  0.0 353.7 jit_solution(9272582506453636841)
XLA Ops:
  7.2 0.0 reduce-scatter.4.cloned.1.call-start
  7.2 12.5 %copy.33 = bf16[32,32,1024]{1,0,2:T(8,128)(2,1)} copy(bf16[32,32,1024]{2,1,0:T(8,128)(2,1)} %bitcast.48) | data formatting | bytes 4194304
  19.7 12.4 %reshape.102 = bf16[1024,1024]{1,0:T(8,128)(2,1)} reshape(bf16[1024,32,32]{2,1,0:T(8,128)(2,1)} %bitcast.43) | data formatting | bytes 4194304
  32.1 0.0 all-gather.5.cloned.1.call-start
  32.2 0.9 copy-done.2
  33.1 23.1 %all_to_all.59 = bf16[32,32,128]{2,1,0:T(8,128)(2,1)} all-to-all(bf16[32,32,128]{2,1,0:T(8,128)(2,1)S(1)} %copy-done.2), channel_id=1, replica_groups=mesh['shard'=32,'tensor'=4,'section'=2] {'shard'}, dimensions={0} | all-to-all | bytes 524288 | tf_op jit(solution)/shard_map/all_to_all | solution.py:82
  56.2 14.5 %reduce-scatter.4.cloned.1.call-done = bf16[128,1024]{1,0:T(8,128)(2,1)} async-done(((bf16[1024,1024]{1,0:T(8,128)(2,1)}), bf16[128,1024]{1,0:T(8,128)(2,1)}) %reduce-scatter.4.cloned.1.call-update) | async-done | bytes 262160
  70.6 1.8 reshape.103
  72.5 1.8 copy.34
  74.2 9.1 %all-to-all-start.1 = ((bf16[32,32,128]{2,1,0:T(8,128)(2,1)}), bf16[32,32,128]{2,1,0:T(8,128)(2,1)S(1)}, u32[]{:S(2)}, u32[]{:S(2)}) async-start(bf16[32,32,128]{2,1,0:T(8,128)(2,1)} %copy.34), calls=%async_computation.1 | async-start | bytes 524288 | tf_op jit(solution)/shard_map/all_to_all | solution.py:82
  83.3 0.0 all-gather.9.cloned.1.call-start
  83.4 19.8 %all-gather.5.cloned.1.call-done = bf16[1,1024,1024]{2,1,0:T(8,128)(2,1)} async-done(((bf16[1,1024,128]{2,1,0:T(8,128)(2,1)}), bf16[1,1024,1024]{2,1,0:T(8,128)(2,1)}) %all-gather.5.cloned.1.call-update) | async-done | bytes 2097168 | tf_op jit(solution)/shard_map/all_gather | solution.py:86
  103.2 3.0 fusion.2
  106.2 9.6 %all-to-all-start.2 = ((bf16[32,32,128]{2,1,0:T(8,128)(2,1)}), bf16[32,32,128]{2,1,0:T(8,128)(2,1)S(1)}, u32[]{:S(2)}, u32[]{:S(2)}) async-start(bf16[32,32,128]{2,1,0:T(8,128)(2,1)} %param.21), calls=%async_computation.2 | async-start | bytes 524288 | tf_op jit(solution)/shard_map/all_to_all | solution.py:82
  115.8 0.2 convert_reduce_fusion
  116.0 0.1 select_reduce_fusion
  116.0 0.1 fusion.13
  116.2 1.7 gather_fusion
  117.8 1.2 select_select_fusion
  119.0 8.4 %all-to-all-done.2 = bf16[32,32,128]{2,1,0:T(8,128)(2,1)S(1)} async-done(((bf16[32,32,128]{2,1,0:T(8,128)(2,1)}), bf16[32,32,128]{2,1,0:T(8,128)(2,1)S(1)}, u32[]{:S(2)}, u32[]{:S(2)}) %all-to-all-start.2) | async-done | bytes 262176 | tf_op jit(solution)/shard_map/all_to_all | solution.py:82
  127.4 4.5 %all-to-all-start.4 = ((bf16[96,32,128]{2,1,0:T(8,128)(2,1)}), bf16[96,32,128]{2,1,0:T(8,128)(2,1)S(1)}, u32[]{:S(2)}, u32[]{:S(2)}) async-start(bf16[96,32,128]{2,1,0:T(8,128)(2,1)} %select_select_fusion), calls=%async_computation.4 | async-start | bytes 1572864 | tf_op jit(solution)/shard_map/all_to_all | solution.py:82
  132.0 4.7 %all-gather.9.cloned.1.call-done = bf16[1024,1024]{1,0:T(8,128)(2,1)} async-done(((bf16[1024,128]{1,0:T(8,128)(2,1)}), bf16[1024,1024]{1,0:T(8,128)(2,1)}) %all-gather.9.cloned.1.call-update) | async-done | bytes 2097168 | tf_op jit(solution)/shard_map/all_gather | solution.py:91
  136.7 2.9 multiply_reduce_fusion
  139.6 0.4 copy.39
  140.0 0.5 broadcast.82
  140.5 2.2 reduce.2
  142.7 0.8 reshape.104
  143.5 9.2 %all-to-all-done.4 = bf16[96,32,128]{2,1,0:T(8,128)(2,1)S(1)} async-done(((bf16[96,32,128]{2,1,0:T(8,128)(2,1)}), bf16[96,32,128]{2,1,0:T(8,128)(2,1)S(1)}, u32[]{:S(2)}, u32[]{:S(2)}) %all-to-all-start.4) | async-done | bytes 786464 | tf_op jit(solution)/shard_map/all_to_all | solution.py:82
  152.7 6.4 %all-to-all-start.3 = ((bf16[32,2,2048]{2,1,0:T(2,128)(2,1)}), bf16[32,2,2048]{2,1,0:T(2,128)(2,1)S(1)}, u32[]{:S(2)}, u32[]{:S(2)}) async-start(bf16[32,2,2048]{2,1,0:T(2,128)(2,1)} %reshape.104), calls=%async_computation.3 | async-start | bytes 524288 | tf_op jit(solution)/shard_map/all_to_all | solution.py:96
  159.0 0.1 copy.29
  159.1 10.2 %all-to-all-done.3 = bf16[32,2,2048]{2,1,0:T(2,128)(2,1)S(1)} async-done(((bf16[32,2,2048]{2,1,0:T(2,128)(2,1)}), bf16[32,2,2048]{2,1,0:T(2,128)(2,1)S(1)}, u32[]{:S(2)}, u32[]{:S(2)}) %all-to-all-start.3) | async-done | bytes 262176 | tf_op jit(solution)/shard_map/all_to_all | solution.py:96
  169.3 4.0 %stack.5 = bf16[8,3,1024,128]{3,2,1,0:T(8,128)(2,1)} broadcast(bf16[3,1024,128]{2,1,0:T(8,128)(2,1)S(1)} %bitcast.45), dimensions={1,2,3} | broadcast | bytes 7077888 | tf_op jit(solution)/shard_map/stack | solution.py:102
  173.3 8.5 %all-to-all-start.5 = ((bf16[8,3,1024,128]{3,2,1,0:T(8,128)(2,1)}), bf16[8,3,1024,128]{3,2,1,0:T(8,128)(2,1)}, u32[]{:S(2)}, u32[]{:S(2)}) async-start(bf16[8,3,1024,128]{3,2,1,0:T(8,128)(2,1)} %stack.5), calls=%async_computation.5 | async-start | bytes 12582912 | tf_op jit(solution)/shard_map/all_to_all | solution.py:101
  181.8 0.6 dynamic_slice.6
  182.4 2.4 multiply_reduce_fusion.1
  184.8 0.1 convert_reduce_fusion.1
  184.9 1.3 compare_select_fusion.2
  186.2 131.5 %all-reduce = (f32[5]{0:T(128)S(1)}, f32[5]{0:T(128)S(1)}) all-reduce(f32[5]{0:T(128)S(1)} %get-tuple-element.9, f32[5]{0:T(128)S(1)} %compare_select_fusion.2), channel_id=1, replica_groups=mesh['shard'=32,'tensor'=4,'section'=2] {'shard','tensor','section'}, use_global_device_ids=true, to_apply=%region_3.0 | all-reduce | flops 10 | bytes 80 | tf_op jit(solution)/shard_map/psum | solution.py:119
  317.7 0.1 select_reduce_fusion.1
  317.8 0.3 reshape.105
  318.1 0.5 bitcast_convert_fusion
  318.7 0.9 fusion.8
  319.6 0.7 multiply_subtract_fusion
  320.3 3.9 %copy_bitcast_fusion = bf16[3,1024,1024]{2,1,0:T(8,128)(2,1)S(1)} fusion(bf16[8,3,1024,128]{3,2,1,0:T(8,128)(2,1)} %all-to-all-done.5), kind=kLoop, calls=%fused_computation.1 | loop fusion | bytes 12582912 | tf_op jit(solution)/shard_map/reshape | solution.py:100
  324.2 3.0 multiply_add_fusion.1
  327.1 6.3 %multiply_add_fusion = f32[3,1024,128]{2,1,0:T(8,128)} fusion(f32[3,1024,128]{2,1,0:T(8,128)S(1)} %copy-done.10, bf16[3,1024,128]{2,1,0:T(8,128)(2,1)S(1)} %bitcast.46, bf16[8,3,1024,128]{3,2,1,0:T(8,128)(2,1)} %all-to-all-done.5), kind=kOutput, calls=%fused_computation.4 | convolution fusion | flops 806486016 | bytes 10223616 | tf_op jit(solution)/shard_map/ski,skj->sij/dot_general | solution.py:114
  333.4 10.6 %all-gather.7.cloned.1.call-done = bf16[32,32,1024]{2,1,0:T(8,128)(2,1)} async-done(((bf16[32,32,128]{2,1,0:T(8,128)(2,1)}), bf16[32,32,1024]{2,1,0:T(8,128)(2,1)}) %all-gather.7.cloned.1.call-update) | async-done | bytes 2097168 | tf_op jit(solution)/shard_map/all_gather | solution.py:132
  344.0 3.2 copy.41
  (35 shorter events, 0.2 us)
Async XLA Ops:
  7.2 63.5 %reduce-scatter.4.cloned.1.call-start = ((), (), s32[]{:S(2)}) async-start(), calls=%async_computation.10 | async-start | bytes 2359296
  32.1 0.9 copy-start.2
  32.1 71.0 %all-gather.5.cloned.1.call-start = ((), (), s32[]{:S(2)}) async-start(), calls=%async_computation.7 | async-start | bytes 2359296 | tf_op jit(solution)/shard_map/all_gather | solution.py:86
  74.2 41.5 %copy-start.11 = (s32[32]{0:T(128)S(1)}, s32[32]{0:T(128)}, u32[]{:S(2)}) copy-start(s32[32]{0:T(128)} %param.22) | copy-start | bytes 388
  74.2 28.9 %all-to-all-start.1 = ((bf16[32,32,128]{2,1,0:T(8,128)(2,1)}), bf16[32,32,128]{2,1,0:T(8,128)(2,1)S(1)}, u32[]{:S(2)}, u32[]{:S(2)}) async-start(bf16[32,32,128]{2,1,0:T(8,128)(2,1)} %copy.34), calls=%async_computation.1 | async-start | bytes 524288 | tf_op jit(solution)/shard_map/all_to_all | solution.py:82
  83.3 53.3 %all-gather.9.cloned.1.call-start = ((), (), s32[]{:S(2)}) async-start(), calls=%async_computation.9 | async-start | bytes 2359296 | tf_op jit(solution)/shard_map/all_gather | solution.py:91
  106.2 21.2 %all-to-all-start.2 = ((bf16[32,32,128]{2,1,0:T(8,128)(2,1)}), bf16[32,32,128]{2,1,0:T(8,128)(2,1)S(1)}, u32[]{:S(2)}, u32[]{:S(2)}) async-start(bf16[32,32,128]{2,1,0:T(8,128)(2,1)} %param.21), calls=%async_computation.2 | async-start | bytes 524288 | tf_op jit(solution)/shard_map/all_to_all | solution.py:82
  127.4 25.2 %all-to-all-start.4 = ((bf16[96,32,128]{2,1,0:T(8,128)(2,1)}), bf16[96,32,128]{2,1,0:T(8,128)(2,1)S(1)}, u32[]{:S(2)}, u32[]{:S(2)}) async-start(bf16[96,32,128]{2,1,0:T(8,128)(2,1)} %select_select_fusion), calls=%async_computation.4 | async-start | bytes 1572864 | tf_op jit(solution)/shard_map/all_to_all | solution.py:82
  152.7 16.6 %all-to-all-start.3 = ((bf16[32,2,2048]{2,1,0:T(2,128)(2,1)}), bf16[32,2,2048]{2,1,0:T(2,128)(2,1)S(1)}, u32[]{:S(2)}, u32[]{:S(2)}) async-start(bf16[32,2,2048]{2,1,0:T(2,128)(2,1)} %reshape.104), calls=%async_computation.3 | async-start | bytes 524288 | tf_op jit(solution)/shard_map/all_to_all | solution.py:96
  173.3 8.5 %copy-start.8 = (s32[32]{0:T(128)S(1)}, s32[32]{0:T(128)}, u32[]{:S(2)}) copy-start(s32[32]{0:T(128)} %param.23) | copy-start | bytes 388
  173.3 9.1 %copy-start = (f32[32,32,128]{2,1,0:T(8,128)S(1)}, f32[32,32,128]{2,1,0:T(8,128)}, u32[]{:S(2)}) copy-start(f32[32,32,128]{2,1,0:T(8,128)} %param.16) | copy-start | bytes 1572868
  173.3 9.1 %copy-start.1 = (f32[32,32,128]{2,1,0:T(8,128)S(1)}, f32[32,32,128]{2,1,0:T(8,128)}, u32[]{:S(2)}) copy-start(f32[32,32,128]{2,1,0:T(8,128)} %param.17) | copy-start | bytes 1572868
  173.3 147.0 %all-to-all-start.5 = ((bf16[8,3,1024,128]{3,2,1,0:T(8,128)(2,1)}), bf16[8,3,1024,128]{3,2,1,0:T(8,128)(2,1)}, u32[]{:S(2)}, u32[]{:S(2)}) async-start(bf16[8,3,1024,128]{3,2,1,0:T(8,128)(2,1)} %stack.5), calls=%async_computation.5 | async-start | bytes 12582912 | tf_op jit(solution)/shard_map/all_to_all | solution.py:101
  181.8 162.2 %all-gather.7.cloned.1.call-start = ((), (), s32[]{:S(2)}) async-start(), calls=%async_computation.8 | async-start | bytes 2359296 | tf_op jit(solution)/shard_map/all_gather | solution.py:132
  182.4 136.3 %copy-start.3 = (bf16[32,32,128]{2,1,0:T(8,128)(2,1)S(1)}, bf16[32,32,128]{2,1,0:T(8,128)(2,1)}, u32[]{:S(2)}) copy-start(bf16[32,32,128]{2,1,0:T(8,128)(2,1)} %param.15) | copy-start | bytes 786436
  184.8 134.8 %copy-start.4 = (f32[26,256]{1,0:T(8,128)S(1)}, f32[26,256]{1,0:T(8,128)}, u32[]{:S(2)}) copy-start(f32[26,256]{1,0:T(8,128)} %param.24) | copy-start | bytes 79876
  184.8 134.8 %copy-start.5 = (f32[26,256]{1,0:T(8,128)S(1)}, f32[26,256]{1,0:T(8,128)}, u32[]{:S(2)}) copy-start(f32[26,256]{1,0:T(8,128)} %param.26) | copy-start | bytes 79876
  184.8 134.8 %copy-start.6 = (f32[26,256]{1,0:T(8,128)S(1)}, f32[26,256]{1,0:T(8,128)}, u32[]{:S(2)}) copy-start(f32[26,256]{1,0:T(8,128)} %param.27) | copy-start | bytes 79876
  184.8 134.8 %copy-start.7 = (bf16[26,256]{1,0:T(8,128)(2,1)S(1)}, bf16[26,256]{1,0:T(8,128)(2,1)}, u32[]{:S(2)}) copy-start(bf16[26,256]{1,0:T(8,128)(2,1)} %param.25) | copy-start | bytes 39940
  320.3 3.9 %copy-start.9 = (f32[3,1024,128]{2,1,0:T(8,128)S(1)}, f32[3,1024,128]{2,1,0:T(8,128)}, u32[]{:S(2)}) copy-start(f32[3,1024,128]{2,1,0:T(8,128)} %param.18) | copy-start | bytes 4718596
  324.1 3.0 copy-start.10
Sparse Core Ops, SparseCore 0:
  32.3 38.3 reduce-scatter.3
  72.5 30.6 all-gather.4
  106.3 30.2 all-gather.8
  319.7 24.2 all-gather.6
